TPU v7x, 32 devices: a whole 2x2x4 slice. The times are simulated.
32 devices in a mesh: owner: 4 (over z), lane: 8 (over y, x, core).
Axes of the slice: x: 2, y: 2, z: 4, core: 2. Of those that a mesh axis runs over, the one named last changes fastest.
Arguments:
- tokens: bfloat16 [16384, 4096], P(('owner', 'lane')), may hold values from -6 to 6
- value_base_weight: bfloat16 [4096, 1024], P('lane'), may hold values from -0.09375 to 0.09375
- adapter_down: bfloat16 [4096, 32768], P(None, ('owner', 'lane')), may hold values from -0.09375 to 0.09375
- adapter_up: bfloat16 [32768, 1024], P(('owner', 'lane')), may hold values from -0.75 to 0.75
- adapter_per_row: int32 [16384], P(('owner', 'lane')), may hold values from 0 to 511, as said below
- frequent_adapter: int32 [8], replicated, may hold values from 0 to 511, as said below
Outputs:
- values_out: bfloat16 [16384, 1024], P(('owner', 'lane'))
Inputs may be any that keep to these rules, and one draw needn't show every extreme that they name: `adapter_per_row`: adapter a belongs to device a // 16 of owner+lane in mesh order. Of the rows of one device, exactly 96 have an adapter not in frequent_adapter, and at most 4 of these belong to any one device; in every draw one device receives exactly 4 such rows from every device. The other rows have hot adapters. `frequent_adapter`: 8 distinct adapters, belonging to distinct devices; adapter 512 - 1 is always one of them.
All inputs are finite; a program needn't handle non-finite values.
Results may differ from a plain program's by a relative error of at most 0.0055.
Values may be sent and summed in bfloat16 or wider, within the bound.
A program may use at most 192 MiB of HBM per device.

v0:
```python
import jax
import jax.numpy as jnp
from jax import lax
from jax.sharding import PartitionSpec as P

ADAPTER_RANK = 64
ADAPTERS_DEVICE = 16
HOT = 8
CAP = 4


ADAPTER_SCALE = 2.0


def from_root(block, axis, source):
    block = jnp.where(lax.axis_index(axis) == source, block, jnp.zeros_like(block))
    return lax.psum(block, axis)


def on_device(
    tokens, value_base_weight, adapter_down, adapter_up, adapter_per_row, frequent_adapter
):
    devices = lax.axis_size(("owner", "lane"))
    width = tokens.shape[1]
    output_width = adapter_up.shape[1]
    base_output = jnp.dot(
        tokens,
        lax.all_gather(value_base_weight, "lane", axis=0, tiled=True),
        preferred_element_type=jnp.float32,
    )
    down_parts = []
    up_parts = []
    for hot_index in range(HOT):
        adapter = frequent_adapter[hot_index]
        root_device = adapter // ADAPTERS_DEVICE
        column_offset = adapter % ADAPTERS_DEVICE * ADAPTER_RANK
        down_matrix_piece = lax.dynamic_slice_in_dim(
            adapter_down, column_offset, ADAPTER_RANK, 1
        ).reshape(-1, 128)
        up_matrix_piece = lax.dynamic_slice_in_dim(adapter_up, column_offset, ADAPTER_RANK, 0)
        down_got, up_got = (
            from_root(down_matrix_piece, ("owner", "lane"), root_device),
            from_root(up_matrix_piece, ("owner", "lane"), root_device),
        )
        down_parts.append(down_got.reshape(width, ADAPTER_RANK))
        up_parts.append(up_got)
    hot_down = jnp.concatenate(down_parts, axis=1)
    hot_up = jnp.concatenate(up_parts, axis=0)
    match = adapter_per_row[:, None] == frequent_adapter[None, :]
    is_hot = jnp.any(match, axis=1)
    column_mask = jnp.repeat(match, ADAPTER_RANK, axis=1)
    hot_shrink = jnp.where(
        column_mask, jnp.dot(tokens, hot_down, preferred_element_type=jnp.float32), 0.0
    ).astype(jnp.bfloat16)
    hot_delta = jnp.dot(hot_shrink, hot_up, preferred_element_type=jnp.float32).astype(jnp.bfloat16)
    owner_dev = adapter_per_row // ADAPTERS_DEVICE
    slot = adapter_per_row % ADAPTERS_DEVICE
    hits = (
        (owner_dev[:, None] == jnp.arange(devices, dtype=jnp.int32)[None, :]) & (~is_hot)[:, None]
    ).astype(jnp.int32)
    ranks = jnp.sum(jnp.cumsum(hits, axis=0) * hits, axis=1) - 1
    position = jnp.where(is_hot, devices * CAP, owner_dev * CAP + ranks)
    send_rows = (
        jnp.zeros((devices * CAP, width), jnp.bfloat16)
        .at[position]
        .set(tokens, mode="drop")
        .reshape(devices, CAP, width)
    )
    send_slots = (
        jnp.full((devices * CAP,), -1.0, jnp.bfloat16)
        .at[position]
        .set(slot.astype(jnp.bfloat16), mode="drop")
        .reshape(devices, CAP)
    )
    arrived = lax.all_to_all(send_rows, ("owner", "lane"), split_axis=0, concat_axis=0, tiled=True)
    arrived_slot = lax.all_to_all(
        send_slots, ("owner", "lane"), split_axis=0, concat_axis=0, tiled=True
    )
    leading = arrived.shape[:-1]
    flattened_rows = arrived.reshape(-1, width)
    labels = arrived_slot.reshape(-1).astype(jnp.int32)
    column_holder = jnp.arange(adapter_down.shape[1], dtype=jnp.int32) // ADAPTER_RANK
    rank_projection = jnp.where(
        column_holder[None, :] == labels[:, None],
        jnp.dot(flattened_rows, adapter_down, preferred_element_type=jnp.float32),
        0.0,
    ).astype(jnp.bfloat16)
    final_output = jnp.dot(rank_projection, adapter_up, preferred_element_type=jnp.float32).astype(
        jnp.bfloat16
    )
    returned = lax.all_to_all(
        final_output.reshape(leading + (output_width,)),
        ("owner", "lane"),
        split_axis=0,
        concat_axis=0,
        tiled=True,
    )
    cold_delta = returned.reshape(devices * CAP, output_width)[
        jnp.minimum(position, devices * CAP - 1)
    ]
    adapter_delta = jnp.where(is_hot[:, None], hot_delta, cold_delta)
    return (base_output + ADAPTER_SCALE * adapter_delta.astype(jnp.float32)).astype(jnp.bfloat16)


def solution(mesh):
    placed = (
        P(("owner", "lane"), None),
        P("lane", None),
        P(None, ("owner", "lane")),
        P(("owner", "lane"), None),
        P(("owner", "lane")),
        P(),
    )
    return jax.shard_map(
        on_device, mesh=mesh, in_specs=placed, out_specs=P(("owner", "lane"), None), check_vma=False
    )
```

profile of v0, /device:TPU:0, one launch (start us, length us, event | category | flops | bytes accessed | tf_op | source)
XLA Modules:
  0.0 307.7 jit_solution(15072462262833803733)
XLA Ops:
  7.4 0.0 all-reduce.3.cloned.1.call-start
  7.4 1.6 fusion.26
  29.1 0.0 copy-start
  29.1 10.0 %dynamic-slice_select_fusion = (bf16[4096,64]{1,0:T(8,128)(2,1)}, bf16[4096,64]{1,0:T(8,128)(2,1)}, bf16[4096,64]{1,0:T(8,128)(2,1)}, bf16[4096,64]{1,0:T(8,128)...) fusion(bf16[4096,1024]{1,0:T(8,128)(2,1)} %param.8, ...), kind=kLoop, calls=%fused_computation.12 | loop fusion | flops 2097152 | bytes 8388648 | tf_op jit(solution)/shard_map/jit(_where)/select_n | solution.py:16
  39.2 0.0 copy-done
  39.2 1.1 dynamic-slice_select_fusion.8
  40.2 0.0 all-reduce.3.cloned.1.call-update
  40.3 0.0 all-gather.2.cloned.1.call-start
  40.3 0.5 all-gather.2.cloned.1.call-update
  40.8 0.0 copy-done.9
  40.9 0.0 copy-done.10
  40.9 0.1 broadcast_compare_fusion
  41.1 1.2 reduce-window.6
  42.2 0.2 slice_reduce_fusion
  42.5 0.1 fusion.12
  42.6 3.8 %scatter_custom_fusion = bf16[128]{0:T(256)(128)(2,1)S(1)} fusion(s32[512]{0:T(512)S(1)} %get-tuple-element.38, bf16[512]{0:T(512)(128)(2,1)S(1)} %get-tuple-element.41, bf16[]{:T(256)} %constant.170.clone.1), kind=kCustom, calls=%fused_computation.75 | custom fusion | bytes 258 | tf_op jit(solution)/shard_map/scatter | solution.py:72
  46.4 0.7 all_to_all.16
  47.1 7.5 %all-to-all-start = ((bf16[32,1,4]{2,1,0:T(2,128)(2,1)}), bf16[32,1,4]{2,1,0:T(2,128)(2,1)S(1)}, u32[]{:S(2)}, u32[]{:S(2)}) async-start(bf16[32,1,4]{2,1,0:T(2,128)(2,1)} %all_to_all.16), calls=%async_computation | async-start | bytes 32768 | tf_op jit(solution)/shard_map/all_to_all | solution.py:76
  54.6 7.9 %scatter_custom_fusion.1 = bf16[128,4096]{1,0:T(8,128)(2,1)S(1)} fusion(s32[512]{0:T(512)S(1)} %get-tuple-element.38, bf16[512,4096]{1,0:T(8,128)(2,1)} %param.6, bf16[]{:T(256)} %constant.166.clone.1), kind=kCustom, calls=%fused_computation.20 | custom fusion | bytes 1049088 | tf_op jit(solution)/shard_map/scatter | solution.py:66
  62.6 1.2 reshape.136
  63.8 0.0 all-to-all-done
  63.8 5.7 %all-to-all-start.1 = ((bf16[32,4,4096]{2,1,0:T(4,128)(2,1)}), bf16[32,4,4096]{2,1,0:T(4,128)(2,1)S(1)}, u32[]{:S(2)}, u32[]{:S(2)}) async-start(bf16[32,4,4096]{2,1,0:T(4,128)(2,1)} %reshape.136), calls=%async_computation.1 | async-start | bytes 2097152 | tf_op jit(solution)/shard_map/all_to_all | solution.py:75
  69.5 0.1 convert_reduce_fusion
  69.6 0.1 reshape.148
  69.7 35.9 %all-to-all-done.1 = bf16[32,4,4096]{2,1,0:T(4,128)(2,1)S(1)} async-done(((bf16[32,4,4096]{2,1,0:T(4,128)(2,1)}), bf16[32,4,4096]{2,1,0:T(4,128)(2,1)S(1)}, u32[]{:S(2)}, u32[]{:S(2)}) %all-to-all-start.1) | async-done | bytes 1048608 | tf_op jit(solution)/shard_map/all_to_all | solution.py:75
  105.6 1.1 reshape.137
  106.7 5.4 %convolution_convert_fusion.1 = bf16[128,1024]{1,0:T(8,128)(2,1)S(1)} fusion(bf16[1024,1024]{1,0:T(8,128)(2,1)S(1)} %copy-done, bf16[128,4096]{1,0:T(8,128)(2,1)} %reshape.137, bf16[4096,1024]{1,0:T(8,128)(2,1)} %param.8, s32[1024]{0:T(1024)S(1)} %add_select_fusion, s32[128]{0:T(128)S(1)} %reshape.148), kind=kOutput, calls=%fused_computation.11 | convolution fusion | flops 1342701568 | bytes 11801088 | tf_op jit(solution)/shard_map/dot_general | solution.py:88
  112.1 0.8 reshape.138
  112.9 4.6 %all-to-all-start.2 = ((bf16[32,4,1024]{2,1,0:T(4,128)(2,1)}), bf16[32,4,1024]{2,1,0:T(4,128)(2,1)S(1)}, u32[]{:S(2)}, u32[]{:S(2)}) async-start(bf16[32,4,1024]{2,1,0:T(4,128)(2,1)} %reshape.138), calls=%async_computation.2 | async-start | bytes 524288 | tf_op jit(solution)/shard_map/all_to_all | solution.py:91
  117.5 13.4 %all-to-all-done.2 = bf16[32,4,1024]{2,1,0:T(4,128)(2,1)S(1)} async-done(((bf16[32,4,1024]{2,1,0:T(4,128)(2,1)}), bf16[32,4,1024]{2,1,0:T(4,128)(2,1)S(1)}, u32[]{:S(2)}, u32[]{:S(2)}) %all-to-all-start.2) | async-done | bytes 262176 | tf_op jit(solution)/shard_map/all_to_all | solution.py:91
  130.9 0.1 reshape.139
  131.0 2.1 gather_fusion
  133.1 139.2 %all-reduce.3.cloned.1.call-done = (bf16[64,1024]{1,0:T(8,128)(2,1)}, bf16[64,1024]{1,0:T(8,128)(2,1)}, bf16[64,1024]{1,0:T(8,128)(2,1)}, bf16[64,1024]{1,0:T(8,...) async-done(((bf16[64,1024]{1,0:T(8,128)(2,1)}, ...) | async-done | bytes 5242896 | tf_op jit(solution)/shard_map/psum | solution.py:17
  272.3 0.0 copy-start.3
  272.3 0.0 copy-start.2
  272.3 0.0 copy-start.1
  272.3 10.9 %concatenate.6 = bf16[4096,512]{1,0:T(8,128)(2,1)} concatenate(bf16[4096,64]{1,0:T(8,128)(2,1)} %get-tuple-element.13, bf16[4096,64]{1,0:T(8,128)(2,1)} %get-tuple-element.14, bf16[4096,64]{1,0:T(8,128)(2,1)} %get-tuple-element.15, bf16[4096,64]{1,0:T(8,128)(2,1)} %get-tuple-element.16, bf16[4096,64]{1,0:T(8,128)(2,1)} %get-tuple-element.17, bf16[4096,64]{1,0:T(8,128)(2,1)} %get-tuple-element.18, ...), dimensions={1} | concatenate | bytes 8388608 | tf_op jit(solution)/shard_map/concatenate | solution.py:47
  283.3 0.0 copy-done.8
  283.3 0.0 copy-done.7
  283.3 0.0 copy-done.6
  283.3 0.0 copy-done.5
  283.4 0.0 copy-done.4
  283.4 0.0 copy-done.3
  283.4 0.0 copy-done.2
  283.5 0.1 broadcast_in_dim.45
  283.6 6.5 %fusion = bf16[512,1024]{1,0:T(8,128)(2,1)S(1)} fusion(bf16[512,1024]{1,0:T(8,128)(2,1)S(1)} %gather_fusion, bf16[512,1024]{1,0:T(8,128)(2,1)S(1)} %constant_dynamic-update-slice_fusion, pred[512]{0:T(512)(128)(4,1)S(1)} %get-tuple-element.40, pred[512,512]{0,1:T(32,128)(4,1)S(1)} %bitcast.43, bf16[4096,512]{1,0:T(8,128)(2,1)} %concatenate.6, ...), kind=kOutput, calls=%fused_computation.5 | convolution fusion | flops 2685927424 | bytes 11796992 | tf_op jit(solution)/shard_map/dot_general | solution.py:55
  290.1 0.0 all-gather.2.cloned.1.call-done
  290.1 10.1 %add_convert_fusion = bf16[512,1024]{1,0:T(8,128)(2,1)} fusion(bf16[512,1024]{1,0:T(8,128)(2,1)S(1)} %fusion, bf16[512,4096]{1,0:T(8,128)(2,1)} %param.6, bf16[4096,1024]{1,0:T(8,128)(2,1)} %all-gather.2.cloned.1.call-done), kind=kOutput, calls=%fused_computation.3 | convolution fusion | flops 4297064448 | bytes 14680064 | tf_op jit(solution)/shard_map/dot_general | solution.py:26
  (24 shorter events, 0.2 us)
Async XLA Ops:
  7.4 264.9 %all-reduce.3.cloned.1.call-start = ((), (), s32[]{:S(2)}) async-start(), calls=%async_computation.4 | async-start | bytes 18874368 | tf_op jit(solution)/shard_map/psum | solution.py:17
  29.1 10.0 %copy-start = (bf16[1024,1024]{1,0:T(8,128)(2,1)S(1)}, bf16[1024,1024]{1,0:T(8,128)(2,1)}, u32[]{:S(2)}) copy-start(bf16[1024,1024]{1,0:T(8,128)(2,1)} %param.9) | copy-start | bytes 6291460
  40.2 0.7 copy-start.9
  40.2 0.7 copy-start.10
  40.3 249.8 %all-gather.2.cloned.1.call-start = ((), (), s32[]{:S(2)}) async-start(), calls=%async_computation.3 | async-start | bytes 9437184 | tf_op jit(solution)/shard_map/all_gather | solution.py:28
  47.1 16.7 %all-to-all-start = ((bf16[32,1,4]{2,1,0:T(2,128)(2,1)}), bf16[32,1,4]{2,1,0:T(2,128)(2,1)S(1)}, u32[]{:S(2)}, u32[]{:S(2)}) async-start(bf16[32,1,4]{2,1,0:T(2,128)(2,1)} %all_to_all.16), calls=%async_computation | async-start | bytes 32768 | tf_op jit(solution)/shard_map/all_to_all | solution.py:76
  63.8 41.8 %all-to-all-start.1 = ((bf16[32,4,4096]{2,1,0:T(4,128)(2,1)}), bf16[32,4,4096]{2,1,0:T(4,128)(2,1)S(1)}, u32[]{:S(2)}, u32[]{:S(2)}) async-start(bf16[32,4,4096]{2,1,0:T(4,128)(2,1)} %reshape.136), calls=%async_computation.1 | async-start | bytes 2097152 | tf_op jit(solution)/shard_map/all_to_all | solution.py:75
  112.9 18.0 %all-to-all-start.2 = ((bf16[32,4,1024]{2,1,0:T(4,128)(2,1)}), bf16[32,4,1024]{2,1,0:T(4,128)(2,1)S(1)}, u32[]{:S(2)}, u32[]{:S(2)}) async-start(bf16[32,4,1024]{2,1,0:T(4,128)(2,1)} %reshape.138), calls=%async_computation.2 | async-start | bytes 524288 | tf_op jit(solution)/shard_map/all_to_all | solution.py:91
  272.3 11.0 %copy-start.8 = (bf16[64,1024]{1,0:T(8,128)(2,1)S(1)}, bf16[64,1024]{1,0:T(8,128)(2,1)}, u32[]{:S(2)}) copy-start(bf16[64,1024]{1,0:T(8,128)(2,1)} %get-tuple-element.5) | copy-start | bytes 393220
  272.3 11.0 %copy-start.7 = (bf16[64,1024]{1,0:T(8,128)(2,1)S(1)}, bf16[64,1024]{1,0:T(8,128)(2,1)}, u32[]{:S(2)}) copy-start(bf16[64,1024]{1,0:T(8,128)(2,1)} %get-tuple-element.6) | copy-start | bytes 393220
  272.3 11.0 %copy-start.6 = (bf16[64,1024]{1,0:T(8,128)(2,1)S(1)}, bf16[64,1024]{1,0:T(8,128)(2,1)}, u32[]{:S(2)}) copy-start(bf16[64,1024]{1,0:T(8,128)(2,1)} %get-tuple-element.7) | copy-start | bytes 393220
  272.3 11.0 %copy-start.5 = (bf16[64,1024]{1,0:T(8,128)(2,1)S(1)}, bf16[64,1024]{1,0:T(8,128)(2,1)}, u32[]{:S(2)}) copy-start(bf16[64,1024]{1,0:T(8,128)(2,1)} %get-tuple-element.8) | copy-start | bytes 393220
  272.3 11.1 %copy-start.4 = (bf16[64,1024]{1,0:T(8,128)(2,1)S(1)}, bf16[64,1024]{1,0:T(8,128)(2,1)}, u32[]{:S(2)}) copy-start(bf16[64,1024]{1,0:T(8,128)(2,1)} %get-tuple-element.9) | copy-start | bytes 393220
  272.3 11.1 %copy-start.3 = (bf16[64,1024]{1,0:T(8,128)(2,1)S(1)}, bf16[64,1024]{1,0:T(8,128)(2,1)}, u32[]{:S(2)}) copy-start(bf16[64,1024]{1,0:T(8,128)(2,1)} %get-tuple-element.10) | copy-start | bytes 393220
  272.3 11.1 %copy-start.2 = (bf16[64,1024]{1,0:T(8,128)(2,1)S(1)}, bf16[64,1024]{1,0:T(8,128)(2,1)}, u32[]{:S(2)}) copy-start(bf16[64,1024]{1,0:T(8,128)(2,1)} %get-tuple-element.11) | copy-start | bytes 393220
  272.3 11.1 %copy-start.1 = (bf16[64,1024]{1,0:T(8,128)(2,1)S(1)}, bf16[64,1024]{1,0:T(8,128)(2,1)}, u32[]{:S(2)}) copy-start(bf16[64,1024]{1,0:T(8,128)(2,1)} %get-tuple-element.12) | copy-start | bytes 393220
Sparse Core Ops, SparseCore 0:
  40.4 231.8 all-reduce.2
Sparse Core Ops, SparseCore 1:
  42.6 72.8 all-gather.1
where the time goes:
time: 309 us; the launch traced here: 308 us
  waiting for transfers between devices  189 us (61%)
  between operations  35.3 us (11%)
  local copies, waits for them, and re-layouts  30.8 us (10%)
  matrix products  22 us (7%)
  starting transfers between devices  17.8 us (6%)
  other arithmetic  12.6 us (4%)
    psum x1, waiting for transfers between devices, from_root(): return lax.psum(block, axis)  139 us
    all_to_all x1, waiting for transfers between devices, on_device(): lax.all_to_all(send_rows, ('owner', 'lane'), split_axis=0, concat_axis=0,...  35.9 us
    all_to_all x1, waiting for transfers between devices, on_device(): lax.all_to_all(final_output.reshape(leading + (output_width,)), ('owner',...  13.4 us
    select_n x2, other arithmetic, from_root(): jnp.where(lax.axis_index(axis) == source, block, jnp.zeros_like(block))  11.1 us
    concatenate x1, local copies, waits for them, and re-layouts, on_device(): hot_down = jnp.concatenate(down_parts, axis=1)  10.9 us
    dot_general x1, matrix products, on_device(): jnp.dot(tokens, lax.all_gather(value_base_weight, 'lane', axis=0, tiled=T...  10.1 us
    scatter x1, local copies, waits for them, and re-layouts, on_device(): send_rows = jnp.zeros((devices * CAP, width), jnp.bfloat16).at[position]....  7.93 us
    all_to_all x1, starting transfers between devices, on_device(): lax.all_to_all(send_slots, ('owner', 'lane'), split_axis=0, concat_axis=0...  7.51 us
  transfers between devices with their start and end apart: 5, of which 3 were waited for; matrix products, arithmetic and copies ran while one was open for 14% of the time, Pallas kernels for 0%

commit v1 on v0

v1 whole, which is shorter than its diff:
```python
import functools

import jax
import jax.numpy as jnp
from jax import lax
from jax.experimental import pallas as pl
from jax.experimental.pallas import tpu as pltpu
from jax.sharding import PartitionSpec as P

ADAPTER_RANK = 64
ADAPTERS_DEVICE = 16
HOT = 8
CAP = 4


ADAPTER_SCALE = 2.0

MESH = pl.DeviceIdType.MESH
ANY = pl.BlockSpec(memory_space=pl.ANY)


def remote(src, dst, send, recv, at):
    return pltpu.make_async_remote_copy(
        src_ref=src, dst_ref=dst, send_sem=send, recv_sem=recv, device_id=at, device_id_type=MESH
    )


def position_of(nl):
    o, l = lax.axis_index("owner"), lax.axis_index("lane")
    return o, l, o * nl + l, (o, l + 1 - 2 * lax.rem(l, 2))


def all_to_all(me, nl, n, pairs, send, recv):
    def copies(k):
        to = lax.rem(me + k, n)
        at = (lax.div(to, nl), lax.rem(to, nl))
        return [
            remote(src(to), dst, send.at[i * n + k], recv.at[i * n + k], at)
            for i, (src, dst) in enumerate(pairs)
        ]

    def start():
        @pl.loop(1, n)
        def _(k):
            for c in copies(k):
                c.start()

    def wait():
        @pl.loop(1, n)
        def _(k):
            for c in copies(k):
                c.wait()

    return start, wait


def exchange_kernel(
    no, nl, w, rows, ups, downs, w_all, got, got_up, got_down,
    a_send, a_recv, w_send, w_recv, f_send, f_recv, local,
):
    n, half = no * nl, nl // 2
    o, l, me, partner = position_of(nl)
    mine = pl.ds(pl.multiple_of(me * 128, 128), 128)
    stay = [
        pltpu.make_async_copy(w, w_all.at[l], local.at[0]),
        pltpu.make_async_copy(rows.at[me], got.at[me], local.at[1]),
        pltpu.make_async_copy(ups.at[me], got_up.at[me], local.at[2]),
        pltpu.make_async_copy(downs.at[me], got_down.at[:, mine], local.at[3]),
    ]
    shards = [
        remote(w, w_all.at[l], w_send.at[j], w_recv.at[j], (o, lax.rem(l + 2 * j, nl)))
        for j in range(1, half)
    ]
    forwards = [remote(w, w_all.at[l], f_send.at[0], f_recv.at[0], partner)]
    for c in shards:
        c.start()
    start, wait = all_to_all(
        me, nl, n,
        [
            (lambda to: rows.at[to], got.at[me]),
            (lambda to: ups.at[to], got_up.at[me]),
            (lambda to: downs.at[to], got_down.at[:, mine]),
        ],
        a_send, a_recv,
    )
    start()
    forwards[0].start()
    for c in stay:
        c.start()
    for j in range(1, half):
        shards[j - 1].wait_recv()
        block = w_all.at[lax.rem(l - 2 * j + nl, nl)]
        forwards.append(remote(block, block, f_send.at[j], f_recv.at[j], partner))
        forwards[-1].start()
    wait()
    for c in shards:
        c.wait_send()
    for c in forwards:
        c.wait()
    for c in stay:
        c.wait()


def gather_kernel(
    no, nl, down, up, back, all_down, all_up, got,
    a_send, a_recv, z_send, z_recv, x_send, x_recv, f_send, f_recv, local,
):
    n, half = no * nl, nl // 2
    o, l, me, partner = position_of(nl)
    pieces = ((down, all_down), (up, all_up))
    stay = [
        pltpu.make_async_copy(down, all_down.at[me], local.at[0]),
        pltpu.make_async_copy(up, all_up.at[me], local.at[1]),
        pltpu.make_async_copy(back.at[me], got.at[me], local.at[2]),
    ]
    columns, planes, forwards = {}, {}, []
    for k in range(1, no):
        columns[k] = [
            remote(a, b.at[me], z_send.at[i * no + k], z_recv.at[i * no + k], (lax.rem(o + k, no), l))
            for i, (a, b) in enumerate(pieces)
        ]
        for c in columns[k]:
            c.start()
    start, wait = all_to_all(
        me, nl, n, [(lambda to: back.at[to], got.at[me])], a_send, a_recv
    )
    start()

    def forward(k, j, parts):
        block = lax.rem(o - k + no, no) * nl + lax.rem(l - 2 * j + nl, nl)
        for i, (a, b) in enumerate(parts):
            s = (i * no + k) * half + j
            src = b.at[block] if a is None else a
            forwards.append(remote(src, b.at[block], f_send.at[s], f_recv.at[s], partner))
            forwards[-1].start()

    for k in range(no):
        if k > 0:
            for c in columns[k]:
                c.wait_recv()
        block = lax.rem(o - k + no, no) * nl + l
        for j in range(1, half):
            planes[k, j] = []
            for i, (a, b) in enumerate(pieces):
                s = (i * no + k) * half + j
                src = a if k == 0 else b.at[block]
                c = remote(src, b.at[block], x_send.at[s], x_recv.at[s], (o, lax.rem(l + 2 * j, nl)))
                c.start()
                planes[k, j].append(c)
        forward(k, 0, [(a if k == 0 else None, b) for a, b in pieces])
    for c in stay:
        c.start()
    for k in range(no):
        for j in range(1, half):
            for c in planes[k, j]:
                c.wait_recv()
            forward(k, j, [(None, b) for _, b in pieces])
    wait()
    for group in list(columns.values()) + list(planes.values()):
        for c in group:
            c.wait_send()
    for c in forwards:
        c.wait()
    for c in stay:
        c.wait()


def dma(count):
    return pltpu.SemaphoreType.DMA((count,))


def on_device(
    no, nl, tokens, value_base_weight, adapter_down, adapter_up, adapter_per_row, frequent_adapter
):
    n, half = no * nl, nl // 2
    bf16, f32 = jnp.bfloat16, jnp.float32
    width = tokens.shape[1]
    output_width = adapter_up.shape[1]
    me = lax.axis_index(("owner", "lane"))
    part = width // n
    pair = part // 2
    up_rows = max(1, ADAPTER_RANK // n)
    up_parts = ADAPTER_RANK // up_rows

    match = adapter_per_row[:, None] == frequent_adapter[None, :]
    is_hot = jnp.any(match, axis=1)
    owner_dev = adapter_per_row // ADAPTERS_DEVICE
    slot = adapter_per_row % ADAPTERS_DEVICE
    hits = (
        (owner_dev[:, None] == jnp.arange(n, dtype=jnp.int32)[None, :]) & (~is_hot)[:, None]
    ).astype(jnp.int32)
    ranks = jnp.sum(jnp.cumsum(hits, axis=0) * hits, axis=1) - 1
    position = jnp.where(is_hot, n * CAP, owner_dev * CAP + ranks)
    here = position[:, None] == jnp.arange(n * CAP, dtype=jnp.int32)[None, :]
    place = here.astype(bf16)
    send_rows = (
        lax.dot_general(place, tokens, (((0,), (0,)), ((), ())), preferred_element_type=f32)
        .astype(bf16)
        .reshape(n, CAP, width)
    )
    send_slots = jnp.max(jnp.where(here, slot[:, None], -1), axis=0).astype(bf16)

    hot_root = frequent_adapter // ADAPTERS_DEVICE
    hot_slot = frequent_adapter % ADAPTERS_DEVICE
    own_slot = jnp.sum(jnp.where(hot_root == me, hot_slot, 0))
    columns = lax.dynamic_slice_in_dim(adapter_down, own_slot // 2 * 128, 128, 1)
    lanes = jnp.arange(128, dtype=jnp.int32)
    pick = (
        lanes[:, None] == own_slot % 2 * ADAPTER_RANK + lanes[None, :] % ADAPTER_RANK
    ).astype(bf16)
    twice = jnp.dot(columns, pick, preferred_element_type=f32).astype(bf16).reshape(n, 2, pair, 128)
    send_down = jnp.where(lanes < ADAPTER_RANK, twice[:, 0], twice[:, 1])
    own_up = lax.dynamic_slice_in_dim(adapter_up, own_slot * ADAPTER_RANK, ADAPTER_RANK, 0)
    own_up = own_up.reshape(up_parts, up_rows, output_width)
    own_up = jnp.concatenate([own_up] * (n // up_parts), axis=0)
    tags = jnp.broadcast_to(
        send_slots.reshape(n, 1, CAP, 1), (n, up_rows, CAP, output_width // CAP)
    ).reshape(n, up_rows, output_width)
    send_up = jnp.concatenate([own_up, tags], axis=1)

    def shape(*dims):
        return jax.ShapeDtypeStruct(dims, bf16)

    base_weight, arrived, arrived_up, arrived_down = pl.pallas_call(
        functools.partial(exchange_kernel, no, nl),
        out_shape=(
            shape(nl, *value_base_weight.shape),
            shape(n, CAP, width),
            shape(n, 2 * up_rows, output_width),
            shape(pair, n * 128),
        ),
        in_specs=[ANY] * 4,
        out_specs=[ANY] * 4,
        scratch_shapes=[dma(3 * n), dma(3 * n), dma(half), dma(half), dma(half), dma(half), dma(4)],
        compiler_params=pltpu.CompilerParams(has_side_effects=True),
    )(value_base_weight, send_rows, send_up, send_down)

    order = jnp.arange(ADAPTER_RANK * HOT, dtype=jnp.int32)
    hot_of = order // up_rows % HOT
    rank_of = order // (up_rows * HOT) * up_rows + order % up_rows
    source = hot_root[hot_of] * 128 + rank_of
    index = jnp.arange(n * 128, dtype=jnp.int32)[:, None]
    halves = [
        jnp.dot(
            arrived_down,
            (index == (source + h * ADAPTER_RANK)[None, :]).astype(bf16),
            preferred_element_type=f32,
        ).astype(bf16)
        for h in range(2)
    ]
    piece_down = jnp.concatenate(halves, axis=0)
    piece_up = arrived_up[hot_root, :up_rows].reshape(HOT * up_rows, output_width)

    labels = arrived_up[:, up_rows].reshape(n, CAP, output_width // CAP)[:, :, 0]
    labels = labels.reshape(-1).astype(jnp.int32)
    column_holder = jnp.arange(adapter_down.shape[1], dtype=jnp.int32) // ADAPTER_RANK
    rank_projection = jnp.where(
        column_holder[None, :] == labels[:, None],
        jnp.dot(arrived.reshape(-1, width), adapter_down, preferred_element_type=f32),
        0.0,
    ).astype(bf16)
    final_output = jnp.dot(rank_projection, adapter_up, preferred_element_type=f32).astype(bf16)

    hot_down, hot_up, returned = pl.pallas_call(
        functools.partial(gather_kernel, no, nl),
        out_shape=(
            shape(n, *piece_down.shape),
            shape(n, *piece_up.shape),
            shape(n, CAP, output_width),
        ),
        in_specs=[ANY] * 3,
        out_specs=[ANY] * 3,
        scratch_shapes=[
            dma(n), dma(n), dma(2 * no), dma(2 * no),
            dma(2 * no * half), dma(2 * no * half), dma(2 * no * half), dma(2 * no * half), dma(3),
        ],
        compiler_params=pltpu.CompilerParams(has_side_effects=True),
    )(piece_down, piece_up, final_output.reshape(n, CAP, output_width))

    hot_down = hot_down.reshape(width, HOT * ADAPTER_RANK)
    hot_up = hot_up[:up_parts].reshape(HOT * ADAPTER_RANK, output_width)
    hot_shrink = jnp.where(
        adapter_per_row[:, None] == frequent_adapter[hot_of][None, :],
        jnp.dot(tokens, hot_down, preferred_element_type=f32),
        0.0,
    ).astype(bf16)
    adapter_delta = (
        jnp.dot(hot_shrink, hot_up, preferred_element_type=f32)
        + jnp.dot(place, returned.reshape(n * CAP, output_width), preferred_element_type=f32)
    ).astype(bf16)
    base_output = jnp.dot(
        tokens, base_weight.reshape(width, output_width), preferred_element_type=f32
    )
    return (base_output + ADAPTER_SCALE * adapter_delta.astype(f32)).astype(bf16)


def solution(mesh):
    placed = (
        P(("owner", "lane"), None),
        P("lane", None),
        P(None, ("owner", "lane")),
        P(("owner", "lane"), None),
        P(("owner", "lane")),
        P(),
    )
    return jax.shard_map(
        functools.partial(on_device, mesh.shape["owner"], mesh.shape["lane"]),
        mesh=mesh, in_specs=placed, out_specs=P(("owner", "lane"), None), check_vma=False,
    )
```

time: 309 us -> 191 us (0.62)
  waiting for transfers between devices: 189 us -> 0 us
  Pallas kernels: 0 us -> 125 us
  between operations: 35.3 us -> 3.51 us
  local copies, waits for them, and re-layouts: 30.8 us -> 10.6 us
  starting transfers between devices: 17.8 us -> 0 us
  matrix products: 22 us -> 32.6 us
  other arithmetic: 12.6 us -> 18.3 us
    psum x1 -> x0, waiting for transfers between devices: 139 us -> none  [from_root(): return lax.psum(block, axis)]
    pallas_call x0 -> x2, Pallas kernels: none -> 125 us  [the longest x1 83 us: on_device(): pl.pallas_call(functools.partial(exchange_kernel, no, nl), out_shape=(sha...]
    all_to_all x3 -> x0, waiting for transfers between devices: 49.3 us -> none  [the longest x1 35.9 us: on_device(): lax.all_to_all(send_rows, ('owner', 'lane'), split_axis=0, concat_axis=0,...]
    all_to_all x3 -> x0, starting transfers between devices: 17.8 us -> none  [the longest x1 7.51 us: on_device(): lax.all_to_all(send_slots, ('owner', 'lane'), split_axis=0, concat_axis=0...]
    scatter x2 -> x0, local copies, waits for them, and re-layouts: 11.7 us -> none  [the longest x1 7.93 us: on_device(): send_rows = jnp.zeros((devices * CAP, width), jnp.bfloat16).at[position]....]
    concatenate x2 -> x0, local copies, waits for them, and re-layouts: 10.9 us -> none  [the longest x1 10.9 us: on_device(): hot_down = jnp.concatenate(down_parts, axis=1)]
    dot_general x3 -> x8, matrix products: 22 us -> 32.6 us  [the longest x1 9.41 us: on_device(): jnp.dot(tokens, base_weight.reshape(width, output_width), preferred_eleme...]
    select_n x3, other arithmetic: 11.1 us -> 1.55 us  [the longest x1 0.85 us: on_device(): send_down = jnp.where(lanes < ADAPTER_RANK, twice[:, 0], twice[:, 1])]
  transfers between devices with their start and end apart: 5 -> 0, of which waited for: 3 -> 0; matrix products, arithmetic and copies ran while one was open for 14% -> 0% of each run, Pallas kernels for 0% -> 0%
where the time goes in v1:
time: 191 us; the launch traced here: 190 us
  Pallas kernels  125 us (65%)
  matrix products  32.6 us (17%)
  other arithmetic  18.3 us (10%)
  local copies, waits for them, and re-layouts  10.6 us (6%)
  between operations  3.51 us (2%)
    pallas_call x1, Pallas kernels, on_device(): pl.pallas_call(functools.partial(exchange_kernel, no, nl), out_shape=(sha...  83 us
    pallas_call x1, Pallas kernels, on_device(): pl.pallas_call(functools.partial(gather_kernel, no, nl), out_shape=(shape...  41.9 us
    dot_general x1, matrix products, on_device(): jnp.dot(tokens, base_weight.reshape(width, output_width), preferred_eleme...  9.41 us
    dot_general x1, matrix products, on_device(): jnp.dot(hot_shrink, hot_up, preferred_element_type=f32)  8.32 us
    dot_general x2, matrix products, on_device(): jnp.dot(arrived_down, (index == (source + h * ADAPTER_RANK)[None, :]).ast...  5.17 us
    dot_general x1, matrix products, on_device(): jnp.dot(rank_projection, adapter_up, preferred_element_type=f32)  4.94 us
    gather x2, other arithmetic, on_device(): frequent_adapter[hot_of][None, :]  4.35 us
    gather x1, other arithmetic, on_device(): source = hot_root[hot_of] * 128 + rank_of  4.31 us

profile of v1, /device:TPU:0, one launch (start us, length us, event | category | flops | bytes accessed | tf_op | source)
XLA Modules:
  0.0 189.9 jit_solution(6981444268860414540)
XLA Ops:
  0.0 0.0 copy-start
  0.0 0.9 compare_reduce_fusion
  1.0 0.7 fusion.46
  1.6 1.3 fusion.48
  6.2 0.7 fusion.53
  6.9 4.3 %compare_select_fusion.4 = s32[512,1]{0,1:T(1,128)S(1)} fusion(s32[]{:T(128)} %bitcast.18, s32[]{:T(128)} %bitcast.19, s32[]{:T(128)} %bitcast.20, s32[]{:T(128)} %bitcast.21, s32[]{:T(128)} %bitcast.22, s32[]{:T(128)} %bitcast.24, s32[]{:T(128)} %bitcast.23), kind=kLoop, calls=%fused_computation.72 | loop fusion | flops 17408 | bytes 2076 | tf_op jit(solution)/shard_map/gather | solution.py:241
  11.2 1.6 fusion.52
  12.9 4.3 %compare_select_fusion.3 = s32[512,1]{0,1:T(1,128)S(1)} fusion(s32[]{:T(128)} %bitcast.9, s32[]{:T(128)} %bitcast.10, s32[]{:T(128)} %bitcast.11, s32[]{:T(128)} %bitcast.12, s32[]{:T(128)} %bitcast.13, s32[]{:T(128)} %bitcast.15, s32[]{:T(128)} %bitcast.14), kind=kLoop, calls=%fused_computation.71 | loop fusion | flops 17408 | bytes 2076 | tf_op jit(solution)/shard_map/gather | solution.py:283
  17.2 1.3 broadcast_add_fusion
  18.5 0.7 add_select_fusion.2
  19.2 1.2 reduce-window.6
  20.4 0.2 slice_reduce_fusion.1
  20.7 0.1 fusion.23
  20.8 0.2 select_reduce_fusion
  21.0 0.1 convert_element_type.62
  21.1 0.1 broadcast_in_dim.64
  21.3 0.1 broadcast_in_dim.66
  21.4 0.0 copy-done
  21.4 0.1 reshape.216
  21.5 0.0 copy-start.1
  21.5 1.0 pad_maximum_fusion.ups
  22.5 2.0 %convolution_convert_fusion = bf16[4096,128]{1,0:T(8,128)(2,1)S(1)} fusion(bf16[4096,1024]{1,0:T(8,128)(2,1)} %param.8, s32[]{:T(128)S(6)} %select_n.154, s32[128]{0:T(128)S(1)} %fusion.44), kind=kOutput, calls=%fused_computation.5 | convolution fusion | flops 134758400 | bytes 2097668 | tf_op jit(solution)/shard_map/dot_general | solution.py:211
  24.5 0.8 fusion.11.downs
  25.3 0.0 copy-done.1
  25.3 0.8 convolution_convert_fusion.1
  26.2 1.2 reshape.215.rows
  27.4 83.0 %shard_map.64 = (bf16[8,512,1024]{2,1,0:T(8,128)(2,1)}, bf16[32,4,4096]{2,1,0:T(4,128)(2,1)}, bf16[32,4,1024]{2,1,0:T(4,128)(2,1)}, bf16[64,4096]{1,0:T(8,128)(2,1)}) custom-call(bf16[512,1024]{1,0:T(8,128)(2,1)} %w.1, bf16[32,4,4096]{2,1,0:T(4,128)(2,1)} %reshape.215.rows, bf16[32,4,1024]{2,1,0:T(4,128)(2,1)} %pad_maximum_fusion.ups, ...), custom_call_target="tpu_custom_call" | custom-call | tf_op jit(solution)/shard_map/pallas_call | solution.py:224
  110.4 0.0 copy-start.2
  110.4 2.6 %fusion.8 = bf16[64,512]{1,0:T(8,128)(2,1)S(1)} fusion(bf16[64,4096]{1,0:T(8,128)(2,1)} %get-tuple-element.13, s32[512]{0:T(512)S(1)} %get-tuple-element.21), kind=kOutput, calls=%fused_computation.18 | convolution fusion | flops 270565376 | bytes 591872 | tf_op jit(solution)/shard_map/dot_general | solution.py:244
  113.0 2.6 %fusion.9 = bf16[64,512]{1,0:T(8,128)(2,1)S(1)} fusion(bf16[64,4096]{1,0:T(8,128)(2,1)} %get-tuple-element.13, s32[512]{0:T(512)S(1)} %get-tuple-element.22), kind=kOutput, calls=%fused_computation.19 | convolution fusion | flops 270565376 | bytes 591872 | tf_op jit(solution)/shard_map/dot_general | solution.py:244
  115.6 0.7 pad_maximum_fusion.1.down
  116.3 0.0 copy-done.2
  116.3 0.4 slice_reduce_fusion
  116.7 0.1 copy.24
  116.7 0.7 gather_fusion
  117.5 0.6 reshape.219.up
  118.1 0.6 convert_reduce_fusion
  118.7 0.1 reshape.225
  118.8 1.3 reshape.220
  120.2 0.0 copy-start.3
  120.2 4.9 %convolution_convert_fusion.2 = bf16[128,1024]{1,0:T(8,128)(2,1)S(1)} fusion(bf16[1024,1024]{1,0:T(8,128)(2,1)S(1)} %copy-done, bf16[128,4096]{1,0:T(8,128)(2,1)S(1)} %reshape.220, bf16[4096,1024]{1,0:T(8,128)(2,1)} %param.8, s32[1024]{0:T(1024)S(1)} %add_select_fusion, s32[128]{0:T(128)S(1)} %reshape.225), kind=kOutput, calls=%fused_computation.17 | convolution fusion | flops 1342701568 | bytes 11801088 | tf_op jit(solution)/shard_map/dot_general | solution.py:262
  125.2 0.8 reshape.221.back
  126.0 41.9 %shard_map.65 = (bf16[32,128,512]{2,1,0:T(8,128)(2,1)}, bf16[32,16,1024]{2,1,0:T(8,128)(2,1)}, bf16[32,4,1024]{2,1,0:T(4,128)(2,1)}) custom-call(bf16[128,512]{1,0:T(8,128)(2,1)} %pad_maximum_fusion.1.down, bf16[16,1024]{1,0:T(8,128)(2,1)} %reshape.219.up, bf16[32,4,1024]{2,1,0:T(4,128)(2,1)} %reshape.221.back), custom_call_target="tpu_custom_call" | custom-call | tf_op jit(solution)/shard_map/pallas_call | solution.py:264
  167.9 1.0 reshape.224
  168.9 1.9 %fusion.18 = f32[512,1024]{0,1:T(8,128)} fusion(bf16[128,1024]{1,0:T(8,128)(2,1)S(1)} %reshape.224, s32[512]{0:T(512)S(1)} %add_select_fusion.4), kind=kOutput, calls=%fused_computation.33 | convolution fusion | flops 134283264 | bytes 2361344 | tf_op jit(solution)/shard_map/dot_general | solution.py:289
  170.9 8.3 %add_convert_fusion = bf16[512,1024]{0,1:T(8,128)(2,1)} fusion(f32[512,1024]{0,1:T(8,128)} %fusion.18, bf16[512,1024]{1,0:T(8,128)(2,1)} %bitcast.86, bf16[4096,512]{1,0:T(8,128)(2,1)} %bitcast.85, bf16[512,4096]{1,0:T(8,128)(2,1)} %param.6, s32[512]{0:T(512)S(1)} %copy-done.3, s32[512]{0:T(512)S(1)} %get-tuple-element.25), kind=kOutput, calls=%fused_computation.11 | convolution fusion | flops 2686189568 | bytes 12587008 | tf_op jit(solution)/shard_map/dot_general | solution.py:288
  179.2 9.4 %fusion.4 = bf16[512,1024]{0,1:T(8,128)(2,1)S(1)} fusion(bf16[512,1024]{0,1:T(8,128)(2,1)} %add_convert_fusion, bf16[4096,1024]{1,0:T(8,128)(2,1)} %bitcast.84, bf16[512,4096]{1,0:T(8,128)(2,1)} %param.6), kind=kOutput, calls=%fused_computation.10 | convolution fusion | flops 4297064448 | bytes 14680064 | tf_op jit(solution)/shard_map/dot_general | solution.py:291
  188.6 1.3 copy.28
  (15 shorter events, 0.2 us)
Async XLA Ops:
  0.0 21.4 %copy-start = (bf16[1024,1024]{1,0:T(8,128)(2,1)S(1)}, bf16[1024,1024]{1,0:T(8,128)(2,1)}, u32[]{:S(2)}) copy-start(bf16[1024,1024]{1,0:T(8,128)(2,1)} %param.9) | copy-start | bytes 6291460
  21.5 3.9 %copy-start.1 = (bf16[512,4096]{1,0:T(8,128)(2,1)S(1)}, bf16[512,4096]{1,0:T(8,128)(2,1)}, u32[]{:S(2)}) copy-start(bf16[512,4096]{1,0:T(8,128)(2,1)} %param.6) | copy-start | bytes 12582916
  110.4 5.8 %copy-start.2 = (bf16[32,4,1024]{2,1,0:T(4,128)(2,1)S(1)}, bf16[32,4,1024]{2,1,0:T(4,128)(2,1)}, u32[]{:S(2)}) copy-start(bf16[32,4,1024]{2,1,0:T(4,128)(2,1)} %get-tuple-element.14) | copy-start | bytes 786436
  120.2 50.7 %copy-start.3 = (s32[512]{0:T(512)S(1)}, s32[512]{0:T(512)}, u32[]{:S(2)}) copy-start(s32[512]{0:T(512)} %param.10) | copy-start | bytes 6148
